TPU v7x, 512 devices: a whole 4x4x16 slice. The times are simulated.
512 devices in a mesh: seq: 128 (over y, z, x_lo), head: 4 (over x_hi, core).
Axes of the slice: x: 4 (x_hi: 2, x_lo: 2; x = x_hi * 2 + x_lo), y: 4, z: 16, core: 2. Of those that a mesh axis runs over, the one named last changes fastest.
Arguments:
- queries: bfloat16 [16384, 1024], P('seq', 'head'), may hold values from -16 to 16
- key_vectors: bfloat16 [16384, 1024], P('seq', 'head'), may hold values from -16 to 16
- values: bfloat16 [16384, 1024], P('seq', 'head'), may hold values from -6 to 6
- step_rates: float32 [16384, 4], P('seq', 'head'), may hold values from 0.1 to 1
- fast_weights: float32 [4, 3, 256, 256], P('head', None, 'seq'), may hold values from -0.375 to 0.375
- momentum: float32 [4, 3, 256, 256], P('head', None, 'seq'), may hold values from -0.4375 to 0.4375
- momentum_decay: float32 [4], P('head'), may hold values from 0.5 to 0.95
- memory_gain: float32 [1024], P('head'), may hold values from 0.5 to 1.5
- window_gain: float32 [1024], P('head'), may hold values from 0.5 to 1.5
Outputs:
- blended: bfloat16 [16384, 1024], P('seq', 'head')
- new_weights: float32 [4, 3, 256, 256], P('head', None, 'seq')
- new_momentum: float32 [4, 3, 256, 256], P('head', None, 'seq')
All inputs are finite; a program needn't handle non-finite values.
Results may differ from a plain program's by a relative error of at most 0.0085.
Values may be sent and summed in bfloat16 or wider, within the bound.
No kernel may reach another device: no remote copies, remote signals or barrier semaphores. Data moves between devices by JAX's collectives and lax.ppermute only.
A program may use at most 64 MiB of HBM per device.

v0:
```python
import math

import jax
import jax.numpy as jnp
from jax import lax
from jax.sharding import PartitionSpec as P

WINDOW = 512


def passed_along(value, axis, steps):
    count = lax.axis_size(axis)
    leading, last = (max(0, -steps), min(count, count - steps))
    return lax.ppermute(value, axis, [(source, source + steps) for source in range(leading, last)])


def silu_slope(field):
    sigmoid_x = jax.nn.sigmoid(field)
    return sigmoid_x * (1.0 + field * (1.0 - sigmoid_x))


def keep_scale(candidate, previous):
    old_rms = jnp.sqrt(jnp.mean(previous * previous, axis=-1, keepdims=True) + 1e-06)
    new_rms = jnp.sqrt(jnp.mean(candidate * candidate, axis=-1, keepdims=True) + 1e-06)
    return candidate * (old_rms / new_rms)


def rms_scale(field, gain):
    return field * lax.rsqrt(jnp.mean(field * field, axis=-1, keepdims=True) + 1e-06) * gain


def contract_rows(left, right):
    return lax.dot_general(
        left, right, (((0,), (0,)), ((), ())), preferred_element_type=jnp.float32
    )


def per_device(
    queries,
    key_vectors,
    values,
    step_rates,
    fast_weights,
    momentum,
    momentum_decay,
    memory_gain,
    window_gain,
):
    tokens_here, head_width = queries.shape
    seq_count = lax.axis_size("seq")
    my_index = lax.axis_index("seq")
    shard_rows = fast_weights.shape[2]
    inner_rate = 0.1 / math.sqrt(tokens_here * seq_count)
    hop_count = -(-WINDOW // tokens_here)
    border = (key_vectors, values)
    earlier = []
    for step_back in range(hop_count):
        earlier.append(passed_along((border[0], border[1]), "seq", step_back + 1))
    context_keys = jnp.concatenate(
        [piece[0] for piece in reversed(earlier)] + [key_vectors], axis=0
    )
    context_values = jnp.concatenate([piece[1] for piece in reversed(earlier)] + [values], axis=0)
    block_rows = min(tokens_here, max(WINDOW, 512))
    scores = lax.dot_general(
        queries, context_keys, (((1,), (1,)), ((), ())), preferred_element_type=jnp.float32
    ) * head_width ** (-0.5)
    query_pos = my_index * tokens_here + 0 + jnp.arange(block_rows, dtype=jnp.int32)
    key_pos = my_index * tokens_here + 0 - WINDOW + jnp.arange(block_rows + WINDOW, dtype=jnp.int32)
    distance = query_pos[:, None] - key_pos[None, :]
    allowed = (key_pos[None, :] >= 0) & (distance >= 0) & (distance < WINDOW)
    scores = jnp.where(allowed, scores, jnp.float32(-1e30))
    row_max = jnp.max(scores, axis=1, keepdims=True)
    weights = jnp.exp(scores - row_max)
    probabilities = (weights / jnp.sum(weights, axis=1, keepdims=True)).astype(jnp.bfloat16)
    attended_blocks = jnp.dot(probabilities, context_values, preferred_element_type=jnp.float32)
    owned = fast_weights[0]
    whole_weights, whole_moment = (
        lax.all_gather(owned, "seq", axis=1, tiled=True),
        lax.all_gather(momentum[0], "seq", axis=1, tiled=True),
    )
    gathered = whole_weights.astype(jnp.bfloat16)
    gate_pre = jnp.dot(key_vectors, gathered[0], preferred_element_type=jnp.float32)
    up_pre = jnp.dot(key_vectors, gathered[1], preferred_element_type=jnp.float32)
    gate_act = jax.nn.silu(gate_pre)
    hidden = (gate_act * up_pre).astype(jnp.bfloat16)
    target_grad = (-(inner_rate * step_rates) * values.astype(jnp.float32)).astype(jnp.bfloat16)
    hidden_grad = lax.dot_general(
        target_grad, gathered[2], (((1,), (1,)), ((), ())), preferred_element_type=jnp.float32
    )
    gate_grad = (hidden_grad * up_pre * silu_slope(gate_pre)).astype(jnp.bfloat16)
    up_grad = (hidden_grad * gate_act).astype(jnp.bfloat16)
    paired = jnp.concatenate([gate_grad, up_grad], axis=1)
    summed_all = lax.psum(
        jnp.concatenate(
            [contract_rows(key_vectors, paired), contract_rows(hidden, target_grad)], axis=1
        ),
        "seq",
    )
    gradient = summed_all.reshape(head_width, 3, head_width).transpose(1, 0, 2)
    moment_full = momentum_decay[0] * whole_moment + gradient
    weight_full = keep_scale(whole_weights - moment_full, whole_weights)
    updated = weight_full.astype(jnp.bfloat16)
    weight_new = lax.dynamic_slice_in_dim(weight_full, my_index * shard_rows, shard_rows, 1)
    moment_new = lax.dynamic_slice_in_dim(moment_full, my_index * shard_rows, shard_rows, 1)
    gate_out = jnp.dot(queries, updated[0], preferred_element_type=jnp.float32)
    up_out = jnp.dot(queries, updated[1], preferred_element_type=jnp.float32)
    inner_act = (jax.nn.silu(gate_out) * up_out).astype(jnp.bfloat16)
    recalled = jnp.dot(inner_act, updated[2], preferred_element_type=jnp.float32)
    blended = (rms_scale(recalled, memory_gain) + rms_scale(attended_blocks, window_gain)).astype(
        jnp.bfloat16
    )
    return (blended, weight_new[None], moment_new[None])


def solution(mesh):
    in_specs = (
        P("seq", "head"),
        P("seq", "head"),
        P("seq", "head"),
        P("seq", "head"),
        P("head", None, "seq", None),
        P("head", None, "seq", None),
        P("head"),
        P("head"),
        P("head"),
    )
    out_specs = (P("seq", "head"), P("head", None, "seq", None), P("head", None, "seq", None))
    return jax.shard_map(
        per_device, mesh=mesh, in_specs=in_specs, out_specs=out_specs, check_vma=False
    )
```

profile of v0, /device:TPU:6, one launch (start us, length us, event | category | flops | bytes accessed | tf_op | source)
XLA Modules:
  0.0 1495.0 jit_solution(17726908105991021037)
XLA Ops:
  7.2 0.0 copy-start
  7.2 0.0 all-reduce.2.cloned.1.call-start
  7.2 5.2 collective-permute-start
  12.4 6.7 collective-permute-start.1
  19.1 3.8 collective-permute-start.2
  22.9 3.1 collective-permute-start.3
  26.0 5.2 collective-permute-start.4
  31.2 0.7 copy.19
  31.9 304.1 %all-gather = f32[1,3,256,256]{3,0,1,2:T(1,128)S(1)} all-gather(f32[1,3,2,256]{3,0,1,2:T(1,128)S(1)} %copy.19), channel_id=2, replica_groups=mesh['seq'=128,'head'=4] {'seq'}, dimensions={2}, use_global_device_ids=true | all-gather | bytes 792576 | tf_op jit(solution)/shard_map/all_gather | solution.py:78
  336.1 0.6 copy-done.6
  336.7 0.2 copy-done.1
  336.9 0.2 fusion.11
  337.0 0.7 copy-done.2
  337.7 0.2 fusion.12
  337.9 0.2 multiply_convert_fusion.2
  338.2 0.3 fusion.22
  338.5 0.2 convolution_bitcast_fusion
  338.7 0.1 pad_maximum_fusion
  338.8 1.2 copy.23
  339.9 0.0 all-reduce.2.cloned.1.call-update
  340.0 0.0 copy-start.3
  340.0 0.7 copy-done.3
  340.7 304.3 %all-gather.1 = f32[1,3,256,256]{3,0,1,2:T(1,128)S(1)} all-gather(f32[1,3,2,256]{3,0,1,2:T(1,128)S(1)} %copy.21), channel_id=3, replica_groups=mesh['seq'=128,'head'=4] {'seq'}, dimensions={2}, use_global_device_ids=true | all-gather | bytes 792576 | tf_op jit(solution)/shard_map/all_gather | solution.py:79
  645.7 0.0 collective-permute-done
  645.7 1.3 collective-permute-start.5
  647.0 0.0 collective-permute-done.1
  647.0 1.3 collective-permute-start.6
  648.3 0.0 collective-permute-done.2
  648.3 1.9 collective-permute-start.7
  650.3 0.0 collective-permute-done.3
  650.3 0.0 collective-permute-done.4
  650.3 0.0 collective-permute-done.5
  650.4 0.0 collective-permute-done.6
  650.4 4.1 collective-permute-done.7
  654.5 0.0 copy-done
  654.5 0.6 fusion.29
  655.2 0.1 fusion.8
  655.3 0.3 multiply_reduce_fusion.1
  655.6 828.2 %all-reduce.2.cloned.1.call-done = f32[3,256,256]{2,1,0:T(8,128)} async-done(((f32[3,256,256]{2,1,0:T(8,128)}), f32[3,256,256]{2,1,0:T(8,128)}) %all-reduce.2.cloned.1.call-update) | async-done | bytes 786448 | tf_op jit(solution)/shard_map/psum | solution.py:93
  1483.8 1.4 fusion.5
  1485.3 0.3 fusion.28
  1485.6 0.2 convolution_bitcast_fusion.2
  1485.7 0.0 copy-start.5
  1485.8 0.4 multiply_reduce_fusion.2
  1486.1 0.6 dynamic-slice_bitcast_fusion
  1486.8 0.0 copy-done.5
  1486.8 0.7 copy-done.4
  1487.4 0.7 add_convert_fusion
  (23 shorter events, 0.2 us)
Async XLA Ops:
  7.2 647.4 %copy-start = (bf16[128,256]{1,0:T(8,128)(2,1)S(1)}, bf16[128,256]{1,0:T(8,128)(2,1)}, u32[]{:S(2)}) copy-start(bf16[128,256]{1,0:T(8,128)(2,1)} %param.9) | copy-start | bytes 196612
  7.2 1476.6 %all-reduce.2.cloned.1.call-start = ((), (), s32[]{:S(2)}) async-start(), calls=%async_computation | async-start | bytes 1572864 | tf_op jit(solution)/shard_map/psum | solution.py:93
  7.2 638.5 %collective-permute-start = (bf16[128,256]{1,0:T(8,128)(2,1)}, bf16[128,256]{1,0:T(8,128)(2,1)S(1)}, u32[]{:S(2)}, u32[]{:S(2)}) collective-permute-start(bf16[128,256]{1,0:T(8,128)(2,1)} %param.10), channel_id=1, source_target_pairs={{0,16},{4,20},{8,24},{12,28},{16,32},{20,36},{24,40},{28,44},{32,4... | collective-permute-start | bytes 196616 | tf_op jit(solution)/shard_map/ppermute | solution.py:14
  12.4 634.6 %collective-permute-start.1 = (bf16[128,256]{1,0:T(8,128)(2,1)}, bf16[128,256]{1,0:T(8,128)(2,1)S(1)}, u32[]{:S(2)}, u32[]{:S(2)}) collective-permute-start(bf16[128,256]{1,0:T(8,128)(2,1)} %param.10), channel_id=1, source_target_pairs={{0,12},{4,16},{8,20},{12,24},{16,28},{20,32},{24,36},{28,40},{32,4... | collective-permute-start | bytes 196616 | tf_op jit(solution)/shard_map/ppermute | solution.py:14
  19.1 629.3 %collective-permute-start.2 = (bf16[128,256]{1,0:T(8,128)(2,1)}, bf16[128,256]{1,0:T(8,128)(2,1)S(1)}, u32[]{:S(2)}, u32[]{:S(2)}) collective-permute-start(bf16[128,256]{1,0:T(8,128)(2,1)} %param.10), channel_id=1, source_target_pairs={{0,8},{4,12},{8,16},{12,20},{16,24},{20,28},{24,32},{28,36},{32,40... | collective-permute-start | bytes 196616 | tf_op jit(solution)/shard_map/ppermute | solution.py:14
  22.9 627.4 %collective-permute-start.3 = (bf16[128,256]{1,0:T(8,128)(2,1)}, bf16[128,256]{1,0:T(8,128)(2,1)S(1)}, u32[]{:S(2)}, u32[]{:S(2)}) collective-permute-start(bf16[128,256]{1,0:T(8,128)(2,1)} %param.10), channel_id=1, source_target_pairs={{0,4},{4,8},{8,12},{12,16},{16,20},{20,24},{24,28},{28,32},{32,36}... | collective-permute-start | bytes 196616 | tf_op jit(solution)/shard_map/ppermute | solution.py:14
  26.0 624.3 %collective-permute-start.4 = (bf16[128,256]{1,0:T(8,128)(2,1)}, bf16[128,256]{1,0:T(8,128)(2,1)S(1)}, u32[]{:S(2)}, u32[]{:S(2)}) collective-permute-start(bf16[128,256]{1,0:T(8,128)(2,1)} %param.11), channel_id=1, source_target_pairs={{0,16},{4,20},{8,24},{12,28},{16,32},{20,36},{24,40},{28,44},{32,4... | collective-permute-start | bytes 196616 | tf_op jit(solution)/shard_map/ppermute | solution.py:14
  336.0 0.7 copy-start.6
  336.0 0.9 copy-start.1
  336.9 0.8 copy-start.2
  340.0 0.7 copy-start.3
  645.7 4.7 collective-permute-start.5
  647.0 3.4 collective-permute-start.6
  648.3 6.2 collective-permute-start.7
  1485.7 1.0 copy-start.5
  1486.8 0.7 copy-start.4
Sparse Core Ops, SparseCore 0:
  340.1 1143.6 all-reduce.1
where the time goes:
time: 1500 us
  waiting for transfers between devices  832 us (55%)
  blocking collectives  608 us (41%)
  starting transfers between devices  28.5 us (2%)
  between operations  15 us (1%)
    psum x1, waiting for transfers between devices, per_device(): lax.psum(jnp.concatenate([contract_rows(key_vectors, paired), contract_ro...  828 us
    all_gather x1, blocking collectives, per_device(): lax.all_gather(momentum[0], 'seq', axis=1, tiled=True)  304 us
    all_gather x1, blocking collectives, per_device(): lax.all_gather(owned, 'seq', axis=1, tiled=True)  304 us
  transfers between devices with their start and end apart: 9, of which 2 were waited for; matrix products, arithmetic and copies ran while one was open for 0% of the time, Pallas kernels for 0%

commit v1 on v0

v1 whole, which is shorter than its diff:
```python
import math

import jax
import jax.numpy as jnp
from jax import lax
from jax.sharding import PartitionSpec as P

WINDOW = 512
Y_SIZE, Z_SIZE, X_SIZE = 4, 16, 2
NEAR_Z = 2
FAR = Z_SIZE // NEAR_Z
NEAR = Y_SIZE * NEAR_Z * X_SIZE
WIDTH = 256


def place(y, z, x):
    return (y * Z_SIZE + z) * X_SIZE + x


NEAR_GROUPS = [
    [
        place(y, k * NEAR_Z + p, x)
        for y in range(Y_SIZE)
        for p in range(NEAR_Z)
        for x in range(X_SIZE)
    ]
    for k in range(FAR)
]
FAR_GROUPS = [
    [place(y, k * NEAR_Z + p, x) for k in range(FAR)]
    for y in range(Y_SIZE)
    for p in range(NEAR_Z)
    for x in range(X_SIZE)
]


def exchange(blocks, groups):
    return lax.all_to_all(blocks, "seq", 0, 0, axis_index_groups=groups, tiled=True)


def spread(block, count, groups):
    return exchange(jnp.broadcast_to(block[None], (count,) + block.shape), groups)


def row_order():
    column = lax.broadcasted_iota(jnp.int32, (WIDTH, WIDTH), 1)
    row = lax.broadcasted_iota(jnp.int32, (WIDTH, WIDTH), 0)
    half, slot = column // 128, column % 128
    near, far = slot // FAR, slot % FAR
    x = near % X_SIZE
    p = (near // X_SIZE) % NEAR_Z
    y = near // (X_SIZE * NEAR_Z)
    device = (y * Z_SIZE + far * NEAR_Z + p) * X_SIZE + x
    return (row == 2 * device + half).astype(jnp.bfloat16)


def matmul(left, right):
    return jnp.dot(left, right, preferred_element_type=jnp.float32)


def matrix_of(whole, index):
    first = whole[:, index * 512 : index * 512 + 256]
    second = whole[:, index * 512 + 256 : index * 512 + 512]
    return jnp.concatenate([first, second], axis=0)


def rows_of(matrices):
    pieces = []
    for matrix in matrices:
        pieces += [matrix[:128], matrix[128:]]
    return jnp.concatenate(pieces, axis=1)


def silu_slope(field):
    sigmoid_x = jax.nn.sigmoid(field)
    return sigmoid_x * (1.0 + field * (1.0 - sigmoid_x))


def keep_scale(candidate, previous):
    old_rms = jnp.sqrt(jnp.mean(previous * previous, axis=-1, keepdims=True) + 1e-06)
    new_rms = jnp.sqrt(jnp.mean(candidate * candidate, axis=-1, keepdims=True) + 1e-06)
    return candidate * (old_rms / new_rms)


def rms_scale(field, gain):
    return field * lax.rsqrt(jnp.mean(field * field, axis=-1, keepdims=True) + 1e-06) * gain


def contract_rows(left, right):
    return lax.dot_general(
        left, right, (((0,), (0,)), ((), ())), preferred_element_type=jnp.float32
    )


def attention(queries, key_vectors, values, my_index):
    tokens_here, head_width = queries.shape
    seq_count = lax.axis_size("seq")
    both = jnp.concatenate([key_vectors, values], axis=0)
    earlier = [
        lax.ppermute(both, "seq", [(i, i + back) for i in range(seq_count - back)])
        for back in range(WINDOW // tokens_here, 0, -1)
    ]
    context_keys = jnp.concatenate([piece[:tokens_here] for piece in earlier] + [key_vectors], axis=0)
    context_values = jnp.concatenate([piece[tokens_here:] for piece in earlier] + [values], axis=0)
    scores = lax.dot_general(
        queries, context_keys, (((1,), (1,)), ((), ())), preferred_element_type=jnp.float32
    ) * head_width ** (-0.5)
    query_pos = my_index * tokens_here + jnp.arange(tokens_here, dtype=jnp.int32)
    key_pos = my_index * tokens_here - WINDOW + jnp.arange(tokens_here + WINDOW, dtype=jnp.int32)
    distance = query_pos[:, None] - key_pos[None, :]
    allowed = (key_pos[None, :] >= 0) & (distance >= 0) & (distance < WINDOW)
    scores = jnp.where(allowed, scores, jnp.float32(-1e30))
    row_max = jnp.max(scores, axis=1, keepdims=True)
    weights = jnp.exp(scores - row_max)
    probabilities = (weights / jnp.sum(weights, axis=1, keepdims=True)).astype(jnp.bfloat16)
    return matmul(probabilities, context_values)


def per_device(
    queries,
    key_vectors,
    values,
    step_rates,
    fast_weights,
    momentum,
    momentum_decay,
    memory_gain,
    window_gain,
):
    tokens_here = queries.shape[0]
    seq_count = lax.axis_size("seq")
    my_index = lax.axis_index("seq")
    my_far = ((my_index // X_SIZE) % Z_SIZE) // NEAR_Z
    inner_rate = 0.1 / math.sqrt(tokens_here * seq_count)
    decay = momentum_decay[0]
    attended = attention(queries, key_vectors, values, my_index)
    order = row_order()
    keys_ordered = matmul(key_vectors, order).astype(jnp.bfloat16)
    queries_ordered = matmul(queries, order).astype(jnp.bfloat16)

    own = jnp.concatenate(
        [fast_weights.reshape(1536), momentum.reshape(1536)]
    ).astype(jnp.bfloat16)
    line = spread(own, FAR, FAR_GROUPS)
    line_weights, line_moment = line[:, :1536], line[:, 1536:]
    whole = spread(line_weights, NEAR, NEAR_GROUPS).reshape(seq_count, 1536)
    gate_w, up_w = matrix_of(whole, 0), matrix_of(whole, 1)
    down_w = matmul(order, matrix_of(whole, 2)).astype(jnp.bfloat16)

    gate_pre = matmul(keys_ordered, gate_w)
    up_pre = matmul(keys_ordered, up_w)
    gate_act = jax.nn.silu(gate_pre)
    hidden = (gate_act * up_pre).astype(jnp.bfloat16)
    target_grad = (-(inner_rate * step_rates) * values.astype(jnp.float32)).astype(jnp.bfloat16)
    hidden_grad = lax.dot_general(
        target_grad, down_w, (((1,), (1,)), ((), ())), preferred_element_type=jnp.float32
    )
    gate_grad = (hidden_grad * up_pre * silu_slope(gate_pre)).astype(jnp.bfloat16)
    up_grad = (hidden_grad * gate_act).astype(jnp.bfloat16)
    hidden_ordered = matmul(hidden, order).astype(jnp.bfloat16)
    partial = rows_of(
        [
            contract_rows(keys_ordered, gate_grad),
            contract_rows(keys_ordered, up_grad),
            contract_rows(hidden_ordered, target_grad),
        ]
    ).astype(jnp.bfloat16)

    near_parts = exchange(partial.reshape(NEAR, FAR, 1536), NEAR_GROUPS)
    near_sum = jnp.sum(near_parts.astype(jnp.float32), axis=0).astype(jnp.bfloat16)
    far_parts = spread(near_sum, FAR, FAR_GROUPS)
    gradient = jnp.sum(far_parts.astype(jnp.float32), axis=0)

    def step(weights, moments, grads):
        count = grads.shape[0]
        weights = weights.astype(jnp.float32).reshape(count, 6, WIDTH)
        moments = moments.astype(jnp.float32).reshape(count, 6, WIDTH)
        moved = decay * moments + grads.reshape(count, 6, WIDTH)
        return keep_scale(weights - moved, weights), moved

    line_new = step(line_weights, line_moment, gradient)[0].astype(jnp.bfloat16)
    own_gradient = lax.dynamic_slice_in_dim(gradient, my_far, 1, 0)
    weight_new, moment_new = step(
        fast_weights.reshape(1, 1536), momentum.reshape(1, 1536), own_gradient
    )

    updated = spread(line_new.reshape(FAR, 1536), NEAR, NEAR_GROUPS).reshape(seq_count, 1536)
    gate_out = matmul(queries_ordered, matrix_of(updated, 0))
    up_out = matmul(queries_ordered, matrix_of(updated, 1))
    inner_act = (jax.nn.silu(gate_out) * up_out).astype(jnp.bfloat16)
    recalled = matmul(matmul(inner_act, order).astype(jnp.bfloat16), matrix_of(updated, 2))
    blended = (rms_scale(recalled, memory_gain) + rms_scale(attended, window_gain)).astype(
        jnp.bfloat16
    )
    return (
        blended,
        weight_new.reshape(fast_weights.shape),
        moment_new.reshape(momentum.shape),
    )


def solution(mesh):
    in_specs = (
        P("seq", "head"),
        P("seq", "head"),
        P("seq", "head"),
        P("seq", "head"),
        P("head", None, "seq", None),
        P("head", None, "seq", None),
        P("head"),
        P("head"),
        P("head"),
    )
    out_specs = (P("seq", "head"), P("head", None, "seq", None), P("head", None, "seq", None))
    return jax.shard_map(
        per_device, mesh=mesh, in_specs=in_specs, out_specs=out_specs, check_vma=False
    )
```

time: 1500 us -> 112 us (0.07)
  waiting for transfers between devices: 832 us -> 24.9 us
  blocking collectives: 608 us -> 28 us
    psum x1 -> x0, waiting for transfers between devices: 828 us -> none  [per_device(): lax.psum(jnp.concatenate([contract_rows(key_vectors, paired), contract_ro...]
    all_gather x2 -> x0, blocking collectives: 608 us -> none  [the longest x1 304 us: per_device(): lax.all_gather(momentum[0], 'seq', axis=1, tiled=True)]
    all_to_all x0 -> x1, blocking collectives: none -> 28 us  [exchange(): lax.all_to_all(blocks, 'seq', 0, 0, axis_index_groups=groups, tiled=True)]
    all_to_all x0 -> x4, starting transfers between devices: none -> 27.1 us  [exchange(): lax.all_to_all(blocks, 'seq', 0, 0, axis_index_groups=groups, tiled=True)]
    all_to_all x0 -> x4, waiting for transfers between devices: none -> 24.9 us  [exchange(): lax.all_to_all(blocks, 'seq', 0, 0, axis_index_groups=groups, tiled=True)]
    ppermute x8 -> x4, starting transfers between devices: 28.5 us -> 11.6 us  [attention(): lax.ppermute(both, 'seq', [(i, i + back) for i in range(seq_count - back)])]
  transfers between devices with their start and end apart: 9 -> 8, of which waited for: 2 -> 3; matrix products, arithmetic and copies ran while one was open for 0% -> 3% of each run, Pallas kernels for 0% -> 0%
where the time goes in v1:
time: 112 us; the launch traced here: 111 us
  starting transfers between devices  38.7 us (35%)
  blocking collectives  28 us (25%)
  waiting for transfers between devices  24.9 us (22%)
  local copies, waits for them, and re-layouts  9.64 us (9%)
  other arithmetic  4.23 us (4%)
  matrix products  3.94 us (4%)
  between operations  1.72 us (2%)
    all_to_all x1, blocking collectives, exchange(): lax.all_to_all(blocks, 'seq', 0, 0, axis_index_groups=groups, tiled=True)  28 us
    all_to_all x4, starting transfers between devices, exchange(): lax.all_to_all(blocks, 'seq', 0, 0, axis_index_groups=groups, tiled=True)  27.1 us
    all_to_all x4, waiting for transfers between devices, exchange(): lax.all_to_all(blocks, 'seq', 0, 0, axis_index_groups=groups, tiled=True)  24.9 us
    ppermute x4, starting transfers between devices, attention(): lax.ppermute(both, 'seq', [(i, i + back) for i in range(seq_count - back)])  11.6 us
    unnamed x29, local copies, waits for them, and re-layouts  6 us
    broadcast_in_dim x5, local copies, waits for them, and re-layouts, spread(): jnp.broadcast_to(block[None], (count,) + block.shape)  2.78 us
  transfers between devices with their start and end apart: 8, of which 3 were waited for; matrix products, arithmetic and copies ran while one was open for 3% of the time, Pallas kernels for 0%

profile of v1, /device:TPU:6, one launch (start us, length us, event | category | flops | bytes accessed | tf_op | source)
XLA Modules:
  0.0 111.2 jit_solution(17491774567180632630)
XLA Ops:
  0.7 0.7 convert.34
  1.4 0.1 multiply_reduce_fusion.3
  1.6 0.5 broadcast.244
  2.1 0.9 reduce.7
  3.1 28.0 %all_to_all.29 = bf16[8,2,1536]{2,1,0:T(2,128)(2,1)S(1)} all-to-all(bf16[8,2,1536]{2,1,0:T(2,128)(2,1)S(1)} %reshape.197), channel_id=1, replica_groups={{0,16,32,48,64,80,96,112},{4,20,36,52,68,84,100,116},{8,24,40,56,72,88,..., dimensions={0} | all-to-all | bytes 98304 | tf_op jit(solution)/shard_map/all_to_all | solution.py:38
  31.2 0.8 broadcast_in_dim.13
  32.0 6.5 %all-to-all-start.1 = ((bf16[16,8,1536]{2,1,0:T(8,128)(2,1)}), bf16[16,8,1536]{2,1,0:T(8,128)(2,1)S(1)}, u32[]{:S(2)}, u32[]{:S(2)}) async-start(bf16[16,8,1536]{2,1,0:T(8,128)(2,1)} %broadcast_in_dim.13), calls=%async_computation.1 | async-start | bytes 786432 | tf_op jit(solution)/shard_map/all_to_all | solution.py:38
  38.5 0.6 copy-done.7
  39.2 0.3 convolution_convert_fusion.4
  39.4 6.5 %all-to-all-done.1 = bf16[16,8,1536]{2,1,0:T(8,128)(2,1)S(1)} async-done(((bf16[16,8,1536]{2,1,0:T(8,128)(2,1)}), bf16[16,8,1536]{2,1,0:T(8,128)(2,1)S(1)}, u32[]{:S(2)}, u32[]{:S(2)}) %all-to-all-start.1) | async-done | bytes 393248 | tf_op jit(solution)/shard_map/all_to_all | solution.py:38
  45.9 0.2 fusion.38
  46.1 0.2 fusion.34
  46.3 0.6 copy-done.1
  47.0 0.4 fusion.2
  47.3 0.2 convolution_convert_fusion.1
  47.6 0.2 convolution_convert_fusion.2
  47.8 0.4 convolution_convert_fusion
  48.2 0.6 fusion.58
  48.9 0.7 fusion.57
  49.5 0.6 fusion.56
  50.2 0.6 fusion.55
  50.8 0.6 fusion.54
  51.4 0.6 fusion.53
  52.1 4.6 %all-to-all-start.2 = ((bf16[16,8,1536]{2,1,0:T(8,128)(2,1)}), bf16[16,8,1536]{2,1,0:T(8,128)(2,1)S(1)}, u32[]{:S(2)}, u32[]{:S(2)}) async-start(bf16[16,8,1536]{2,1,0:T(8,128)(2,1)} %fusion.53), calls=%async_computation.2 | async-start | bytes 786432 | tf_op jit(solution)/shard_map/all_to_all | solution.py:38
  56.7 2.4 %collective-permute-start = (bf16[256,256]{1,0:T(8,128)(2,1)S(1)}, bf16[256,256]{1,0:T(8,128)(2,1)S(1)}, u32[]{:S(2)}, u32[]{:S(2)}) collective-permute-start(bf16[256,256]{1,0:T(8,128)(2,1)S(1)} %constant_dynamic-update-slice_fusion), channel_id=1, source_target_pairs={{0,16},{4,20},{8,24},{12,28},{16,32},{20,36},{24,40},{28,44},{32,4... | collective-permute-start | bytes 393224 | tf_op jit(solution)/shard_map/ppermute | solution.py:100
  59.1 2.1 %collective-permute-start.1 = (bf16[256,256]{1,0:T(8,128)(2,1)S(1)}, bf16[256,256]{1,0:T(8,128)(2,1)S(1)}, u32[]{:S(2)}, u32[]{:S(2)}) collective-permute-start(bf16[256,256]{1,0:T(8,128)(2,1)S(1)} %constant_dynamic-update-slice_fusion), channel_id=1, source_target_pairs={{0,12},{4,16},{8,20},{12,24},{16,28},{20,32},{24,36},{28,40},{32,4... | collective-permute-start | bytes 393224 | tf_op jit(solution)/shard_map/ppermute | solution.py:100
  61.2 3.7 %collective-permute-start.2 = (bf16[256,256]{1,0:T(8,128)(2,1)S(1)}, bf16[256,256]{1,0:T(8,128)(2,1)S(1)}, u32[]{:S(2)}, u32[]{:S(2)}) collective-permute-start(bf16[256,256]{1,0:T(8,128)(2,1)S(1)} %constant_dynamic-update-slice_fusion), channel_id=1, source_target_pairs={{0,8},{4,12},{8,16},{12,20},{16,24},{20,28},{24,32},{28,36},{32,40... | collective-permute-start | bytes 393224 | tf_op jit(solution)/shard_map/ppermute | solution.py:100
  64.9 3.4 %collective-permute-start.3 = (bf16[256,256]{1,0:T(8,128)(2,1)S(1)}, bf16[256,256]{1,0:T(8,128)(2,1)S(1)}, u32[]{:S(2)}, u32[]{:S(2)}) collective-permute-start(bf16[256,256]{1,0:T(8,128)(2,1)S(1)} %constant_dynamic-update-slice_fusion), channel_id=1, source_target_pairs={{0,4},{4,8},{8,12},{12,16},{16,20},{20,24},{24,28},{28,32},{32,36}... | collective-permute-start | bytes 393224 | tf_op jit(solution)/shard_map/ppermute | solution.py:100
  68.3 0.3 convolution_convert_fusion.5
  69.4 0.7 broadcast_in_dim.14
  70.1 7.7 %all-to-all-start.3 = ((bf16[8,8,1536]{2,1,0:T(8,128)(2,1)}), bf16[8,8,1536]{2,1,0:T(8,128)(2,1)S(1)}, u32[]{:S(2)}, u32[]{:S(2)}) async-start(bf16[8,8,1536]{2,1,0:T(8,128)(2,1)} %broadcast_in_dim.14), calls=%async_computation.3 | async-start | bytes 393216 | tf_op jit(solution)/shard_map/all_to_all | solution.py:38
  77.9 14.1 %all-to-all-done.3 = bf16[8,8,1536]{2,1,0:T(8,128)(2,1)S(1)} async-done(((bf16[8,8,1536]{2,1,0:T(8,128)(2,1)}), bf16[8,8,1536]{2,1,0:T(8,128)(2,1)S(1)}, u32[]{:S(2)}, u32[]{:S(2)}) %all-to-all-start.3) | async-done | bytes 196640 | tf_op jit(solution)/shard_map/all_to_all | solution.py:38
  92.0 0.1 reduce_sum.87
  92.3 0.8 broadcast_in_dim.15
  93.1 8.3 %all-to-all-start.4 = ((bf16[16,8,1536]{2,1,0:T(8,128)(2,1)}), bf16[16,8,1536]{2,1,0:T(8,128)(2,1)S(1)}, u32[]{:S(2)}, u32[]{:S(2)}) async-start(bf16[16,8,1536]{2,1,0:T(8,128)(2,1)} %broadcast_in_dim.15), calls=%async_computation.4 | async-start | bytes 786432 | tf_op jit(solution)/shard_map/all_to_all | solution.py:38
  101.4 0.6 fusion.86
  102.1 0.1 fusion.7
  102.2 0.3 multiply_reduce_fusion
  102.6 0.7 copy-done.3
  103.3 0.6 multiply_reduce_fusion.2
  103.9 0.7 broadcast_multiply_fusion
  104.6 4.3 %all-to-all-done.4 = bf16[16,8,1536]{2,1,0:T(8,128)(2,1)S(1)} async-done(((bf16[16,8,1536]{2,1,0:T(8,128)(2,1)}), bf16[16,8,1536]{2,1,0:T(8,128)(2,1)S(1)}, u32[]{:S(2)}, u32[]{:S(2)}) %all-to-all-start.4) | async-done | bytes 393248 | tf_op jit(solution)/shard_map/all_to_all | solution.py:38
  108.9 0.2 fusion.42
  109.1 0.2 fusion.3
  109.3 0.4 multiply_reduce_fusion.1
  109.7 0.2 copy-done.6
  110.0 0.4 copy-done.5
  110.4 0.7 add_convert_fusion
  (53 shorter events, 0.8 us)
Async XLA Ops:
  0.6 67.7 %copy-start = (bf16[128,256]{1,0:T(8,128)(2,1)S(1)}, bf16[128,256]{1,0:T(8,128)(2,1)}, u32[]{:S(2)}) copy-start(bf16[128,256]{1,0:T(8,128)(2,1)} %param.9) | copy-start | bytes 196612
  0.6 0.8 copy-start.4
  31.9 7.2 %copy-start.2 = (bf16[128,256]{1,0:T(8,128)(2,1)S(1)}, bf16[128,256]{1,0:T(8,128)(2,1)}, u32[]{:S(2)}) copy-start(bf16[128,256]{1,0:T(8,128)(2,1)} %param.10) | copy-start | bytes 196612
  32.0 13.9 %all-to-all-start.1 = ((bf16[16,8,1536]{2,1,0:T(8,128)(2,1)}), bf16[16,8,1536]{2,1,0:T(8,128)(2,1)S(1)}, u32[]{:S(2)}, u32[]{:S(2)}) async-start(bf16[16,8,1536]{2,1,0:T(8,128)(2,1)} %broadcast_in_dim.13), calls=%async_computation.1 | async-start | bytes 786432 | tf_op jit(solution)/shard_map/all_to_all | solution.py:38
  38.5 0.7 copy-start.7
  46.1 0.8 copy-start.1
  52.1 17.2 %all-to-all-start.2 = ((bf16[16,8,1536]{2,1,0:T(8,128)(2,1)}), bf16[16,8,1536]{2,1,0:T(8,128)(2,1)S(1)}, u32[]{:S(2)}, u32[]{:S(2)}) async-start(bf16[16,8,1536]{2,1,0:T(8,128)(2,1)} %fusion.53), calls=%async_computation.2 | async-start | bytes 786432 | tf_op jit(solution)/shard_map/all_to_all | solution.py:38
  56.7 12.6 %collective-permute-start = (bf16[256,256]{1,0:T(8,128)(2,1)S(1)}, bf16[256,256]{1,0:T(8,128)(2,1)S(1)}, u32[]{:S(2)}, u32[]{:S(2)}) collective-permute-start(bf16[256,256]{1,0:T(8,128)(2,1)S(1)} %constant_dynamic-update-slice_fusion), channel_id=1, source_target_pairs={{0,16},{4,20},{8,24},{12,28},{16,32},{20,36},{24,40},{28,44},{32,4... | collective-permute-start | bytes 393224 | tf_op jit(solution)/shard_map/ppermute | solution.py:100
  59.1 18.7 %collective-permute-start.1 = (bf16[256,256]{1,0:T(8,128)(2,1)S(1)}, bf16[256,256]{1,0:T(8,128)(2,1)S(1)}, u32[]{:S(2)}, u32[]{:S(2)}) collective-permute-start(bf16[256,256]{1,0:T(8,128)(2,1)S(1)} %constant_dynamic-update-slice_fusion), channel_id=1, source_target_pairs={{0,12},{4,16},{8,20},{12,24},{16,28},{20,32},{24,36},{28,40},{32,4... | collective-permute-start | bytes 393224 | tf_op jit(solution)/shard_map/ppermute | solution.py:100
  61.2 16.7 %collective-permute-start.2 = (bf16[256,256]{1,0:T(8,128)(2,1)S(1)}, bf16[256,256]{1,0:T(8,128)(2,1)S(1)}, u32[]{:S(2)}, u32[]{:S(2)}) collective-permute-start(bf16[256,256]{1,0:T(8,128)(2,1)S(1)} %constant_dynamic-update-slice_fusion), channel_id=1, source_target_pairs={{0,8},{4,12},{8,16},{12,20},{16,24},{20,28},{24,32},{28,36},{32,40... | collective-permute-start | bytes 393224 | tf_op jit(solution)/shard_map/ppermute | solution.py:100
  64.9 13.0 %collective-permute-start.3 = (bf16[256,256]{1,0:T(8,128)(2,1)S(1)}, bf16[256,256]{1,0:T(8,128)(2,1)S(1)}, u32[]{:S(2)}, u32[]{:S(2)}) collective-permute-start(bf16[256,256]{1,0:T(8,128)(2,1)S(1)} %constant_dynamic-update-slice_fusion), channel_id=1, source_target_pairs={{0,4},{4,8},{8,12},{12,16},{16,20},{20,24},{24,28},{28,32},{32,36}... | collective-permute-start | bytes 393224 | tf_op jit(solution)/shard_map/ppermute | solution.py:100
  70.1 21.9 %all-to-all-start.3 = ((bf16[8,8,1536]{2,1,0:T(8,128)(2,1)}), bf16[8,8,1536]{2,1,0:T(8,128)(2,1)S(1)}, u32[]{:S(2)}, u32[]{:S(2)}) async-start(bf16[8,8,1536]{2,1,0:T(8,128)(2,1)} %broadcast_in_dim.14), calls=%async_computation.3 | async-start | bytes 393216 | tf_op jit(solution)/shard_map/all_to_all | solution.py:38
  93.1 15.8 %all-to-all-start.4 = ((bf16[16,8,1536]{2,1,0:T(8,128)(2,1)}), bf16[16,8,1536]{2,1,0:T(8,128)(2,1)S(1)}, u32[]{:S(2)}, u32[]{:S(2)}) async-start(bf16[16,8,1536]{2,1,0:T(8,128)(2,1)} %broadcast_in_dim.15), calls=%async_computation.4 | async-start | bytes 786432 | tf_op jit(solution)/shard_map/all_to_all | solution.py:38
  102.6 0.7 copy-start.3
  109.3 0.7 copy-start.6
  109.7 0.7 copy-start.5
